TPU v7x, 256 devices: a whole 4x4x8 slice. The times are simulated.
256 devices in a mesh: set: 8 (over y_hi, x), exp: 4 (over y_lo, core), seq: 8 (over z).
Axes of the slice: x: 4, y: 4 (y_hi: 2, y_lo: 2; y = y_hi * 2 + y_lo), z: 8, core: 2. Of those that a mesh axis runs over, the one named last changes fastest.
Arguments:
- tokens: bfloat16 [12288, 2560], P(('set', 'exp', 'seq')), parts along dimension 0, may hold values from -6 to 6
- expert_ids: int32 [12288, 2], P(('set', 'exp', 'seq')), parts along dimension 0, may hold values from 0 to 3, as said below
- gate_nums: int32 [12288, 2], P(('set', 'exp', 'seq')), parts along dimension 0, may hold values from 1 to 8
- moe_gain: float32 [2560], replicated, may hold values from 0.1 to 1.9
- w_gate_up: bfloat16 [4, 2560, 2, 3584], P('exp', None, None, 'seq'), may hold values from -0.125 to 0.125
- w_down: bfloat16 [4, 3584, 2560], P('exp', 'seq'), may hold values from -0.09375 to 0.09375
- attn_gain: float32 [2560], replicated, may hold values from 0.1 to 1.9
- w_qkv: bfloat16 [2560, 3, 2048], P(None, None, 'seq'), may hold values from -0.125 to 0.125
- q_gain: float32 [128], replicated, may hold values from 1.2 to 2.2
- k_gain: float32 [128], replicated, may hold values from 1.2 to 2.2
- w_out: bfloat16 [2048, 2560], P('seq'), may hold values from -0.125 to 0.125
Outputs:
- mixed: bfloat16 [12288, 2560], P(('set', 'exp', 'seq')), parts along dimension 0
- attended: bfloat16 [12288, 2560], P(('set', 'exp', 'seq')), parts along dimension 0
There are 8 independent parts, one for each index of `set`. A program takes and returns all parts, laid end to end along the dimension named above; an argument that names none is the same for every part. Nothing has to cross between parts.
Inputs may be any that keep to these rules, and one draw needn't show every extreme that they name: `expert_ids`: the two ids of a row differ. In the rows of one device no expert is named by more than 36 rows, and one expert, the same for all devices of a set, is named by exactly 36 of them.
All inputs are finite; a program needn't handle non-finite values.
Results may differ from a plain program's by a relative error of at most 0.014.
Values may be sent and summed in bfloat16 or wider, within the bound.
No kernel may reach another device: no remote copies, remote signals or barrier semaphores. Data moves between devices by JAX's collectives and lax.ppermute only.
A program may use at most 64 MiB of HBM per device.

v0:
```python
import math
import jax
import jax.numpy as jnp
from jax import lax
from jax.sharding import Mesh
from jax.sharding import PartitionSpec as P

EXPERTS = 4
CAP = 36
EXP = ("exp_0", "exp_1")
SET_EXP_SEQ = ("set", "exp_0", "exp_1", "seq")


def cut_along(value, dim, length):
    before, after = (value.shape[:dim], value.shape[dim + 1 :])
    return jnp.moveaxis(value.reshape(*before, length, -1, *after), dim, 0)


def joined_along(pieces, dim):
    lengths = list(pieces.shape[1:])
    lengths[dim] *= pieces.shape[0]
    return jnp.moveaxis(pieces, 0, dim).reshape(lengths)


def moved_by_axis(pieces, axes, order):
    inside = pieces.shape[1:]
    filled = pieces.reshape(*(lax.axis_size(a) for a in axes), *inside)
    for k in order:
        filled = lax.all_to_all(filled, axes[k], k, k, tiled=True)
    return filled.reshape(-1, *inside)


def two_step_exchange(value, groups, order, split_dim, concat_dim):
    length = lax.axis_size(groups[0]) * lax.axis_size(groups[1])
    pieces = cut_along(value, split_dim, length)
    return joined_along(moved_by_axis(pieces, groups, order), concat_dim)


def from_everyone(value, axis):
    length = lax.axis_size(axis)
    return lax.all_to_all(
        jnp.broadcast_to(value[None], (length, *value.shape)), axis, 0, 0, tiled=True
    )


def gather_directly(value, axis, dim):
    return joined_along(from_everyone(value, axis), dim)


def summed_on_arrival(value, axis, dim):
    length = lax.axis_size(axis)
    pieces = lax.all_to_all(cut_along(value, dim, length), axis, 0, 0, tiled=True)
    return jnp.sum(pieces.astype(jnp.float32), axis=0)


def rms_scale(values, gain):
    return values * lax.rsqrt(jnp.mean(values * values, axis=-1, keepdims=True) + 1e-06) * gain


def shards(
    tokens,
    expert_ids,
    gate_nums,
    moe_gain,
    w_gate_up,
    w_down,
    attn_gain,
    w_qkv,
    q_gain,
    k_gain,
    w_out,
):
    tok_rows = tokens.shape[0]
    model_dim = tokens.shape[1]
    tokens_wide = tokens.astype(jnp.float32)
    normed = rms_scale(tokens_wide, moe_gain).astype(jnp.bfloat16)
    flat_ids = expert_ids.reshape(-1)
    onehot = (flat_ids[:, None] == jnp.arange(EXPERTS)[None, :]).astype(jnp.int32)
    before = jnp.cumsum(onehot, axis=0) - onehot
    slot_index = jnp.sum(before * onehot, axis=1)
    destination = flat_ids * CAP + slot_index
    source_rows = normed[jnp.arange(2 * tok_rows) // 2]
    dispatch = jnp.zeros((EXPERTS * CAP, model_dim), jnp.bfloat16).at[destination].set(source_rows)
    dispatch = dispatch.reshape(EXPERTS, CAP, model_dim)
    received = two_step_exchange(dispatch, ("exp_0", "exp_1"), (1, 0), 0, 0)
    gate_up = jnp.einsum(
        "...d,dgf->...gf",
        lax.all_gather(received[None], "seq", axis=0, tiled=True),
        w_gate_up[0],
        preferred_element_type=jnp.float32,
    )
    hidden_all = (jax.nn.silu(gate_up[..., 0, :]) * gate_up[..., 1, :]).astype(jnp.bfloat16)
    summed = lax.psum_scatter(
        jnp.einsum(
            "...f,fd->...d", hidden_all, w_down[0], preferred_element_type=jnp.float32
        ).astype(jnp.bfloat16),
        "seq",
        scatter_dimension=0,
        tiled=True,
    ).astype(jnp.float32)
    expert_out = lax.all_to_all(
        summed[0].astype(jnp.bfloat16), EXP, split_axis=0, concat_axis=0, tiled=True
    ).astype(jnp.float32)
    picked = expert_out.reshape(EXPERTS * CAP, model_dim)[destination].reshape(
        tok_rows, 2, model_dim
    )
    nums = gate_nums.astype(jnp.float32)
    weights = nums / jnp.sum(nums, axis=1, keepdims=True)
    moe_total = jnp.sum(weights[:, :, None] * picked, axis=1)
    mixed = (tokens_wide + moe_total).astype(jnp.bfloat16)
    mixed_wide = mixed.astype(jnp.float32)
    attn_in = rms_scale(mixed_wide, attn_gain).astype(jnp.bfloat16)
    head_size = q_gain.shape[0]
    local_heads = w_qkv.shape[2] // head_size
    piece = gather_directly(attn_in, "seq", 0)
    qkv = jnp.einsum("nd,dgc->ngc", piece, w_qkv, preferred_element_type=jnp.float32)
    qkv = qkv.reshape(piece.shape[0], 3, local_heads, head_size)
    queries = rms_scale(qkv[:, 0], q_gain)
    keys_part = rms_scale(qkv[:, 1], k_gain)
    stacked = jnp.stack([queries, keys_part, qkv[:, 2]], axis=1)
    projected = stacked.reshape(piece.shape[0], 3, local_heads * head_size).astype(jnp.bfloat16)
    query_count = projected.shape[0]
    query_heads = projected[:, 0].reshape(query_count, local_heads, head_size)
    scale_factor = 1.0 / math.sqrt(head_size)
    key_piece = lax.all_gather(projected[:, 1], EXP, axis=0, tiled=True)
    value_piece = lax.all_gather(projected[:, 2], EXP, axis=0, tiled=True)
    key_heads = key_piece.reshape(key_piece.shape[0], local_heads, head_size)
    value_heads = value_piece.reshape(value_piece.shape[0], local_heads, head_size)
    scores = (
        jnp.einsum("qhc,khc->qhk", query_heads, key_heads, preferred_element_type=jnp.float32)
        * scale_factor
    )
    probs = jnp.exp(scores)
    denom = jnp.sum(probs, axis=-1)
    numer = jnp.einsum(
        "qhk,khc->qhc", probs.astype(jnp.bfloat16), value_heads, preferred_element_type=jnp.float32
    )
    numer, denom = (numer, denom)
    heads_out = (
        (numer / denom[:, :, None])
        .astype(jnp.bfloat16)
        .reshape(query_count, local_heads * head_size)
    )
    attn_rows = summed_on_arrival(
        jnp.dot(heads_out, w_out, preferred_element_type=jnp.float32).astype(jnp.bfloat16), "seq", 0
    )
    attended = (mixed_wide + attn_rows).astype(jnp.bfloat16)
    return (mixed, attended)


def solution(mesh):
    torus = Mesh(
        mesh.devices.reshape(mesh.shape["set"], 2, 2, mesh.shape["seq"]),
        ("set", "exp_0", "exp_1", "seq"),
    )
    in_specs = (
        P(SET_EXP_SEQ, None),
        P(SET_EXP_SEQ, None),
        P(SET_EXP_SEQ, None),
        P(),
        P(EXP, None, None, "seq"),
        P(EXP, "seq", None),
        P(),
        P(None, None, "seq"),
        P(),
        P(),
        P("seq", None),
    )
    out_specs = (P(SET_EXP_SEQ, None), P(SET_EXP_SEQ, None))
    return jax.shard_map(
        shards, mesh=torus, in_specs=in_specs, out_specs=out_specs, check_vma=False
    )
```

profile of v0, /device:TPU:1, one launch (start us, length us, event | category | flops | bytes accessed | tf_op | source)
XLA Modules:
  0.0 367.5 jit_solution(4428204008842671317)
XLA Ops:
  7.2 0.9 copy.38
  9.6 1.1 fusion.12
  10.7 1.1 fusion.14
  11.8 3.7 %scatter_custom_fusion = bf16[144,2560]{1,0:T(8,128)(2,1)} fusion(s32[96]{0:T(128)S(1)} %fusion.30, bf16[48,2560]{1,0:T(8,128)(2,1)S(1)} %fusion.14, s32[1024]{0:T(1024)S(1)} %pad_clamp_fusion.1, bf16[]{:T(256)} %constant.36.clone.1), kind=kCustom, calls=%fused_computation.36 | custom fusion | bytes 737282 | tf_op jit(solution)/shard_map/scatter | solution.py:83
  15.5 1.3 reshape_reshape_reshape.3
  16.8 0.8 copy.39
  17.5 7.1 %all_to_all.25 = bf16[2,2,1,36,2560]{4,0,3,2,1:T(2,128)(2,1)S(1)} all-to-all(bf16[2,2,1,36,2560]{4,0,3,2,1:T(2,128)(2,1)S(1)} %copy.39), channel_id=1, replica_groups=mesh['set'=8,'exp_0'=2,'exp_1'=2,'seq'=8] {'exp_1'}, dimensions={1} | all-to-all | bytes 1474560 | tf_op jit(solution)/shard_map/all_to_all | solution.py:29
  25.2 12.4 %all_to_all.26 = bf16[2,2,1,36,2560]{4,1,3,2,0:T(2,128)(2,1)S(1)} all-to-all(bf16[2,2,1,36,2560]{4,1,3,2,0:T(2,128)(2,1)S(1)} %copy.40), channel_id=1, replica_groups=mesh['set'=8,'exp_0'=2,'exp_1'=2,'seq'=8] {'exp_0'}, dimensions={0} | all-to-all | bytes 1474560 | tf_op jit(solution)/shard_map/all_to_all | solution.py:29
  38.1 1.2 broadcast_in_dim_reshape_reshape.3
  39.4 72.5 %all-gather.2.cloned.1.call-done = bf16[8,4,36,2560]{3,1,2,0:T(4,128)(2,1)} async-done(((bf16[1,4,36,2560]{3,1,2,0:T(4,128)(2,1)}), bf16[8,4,36,2560]{3,1,2,0:T(4,128)(2,1)}) %all-gather.2.cloned.1.call-update) | async-done | bytes 5898256 | tf_op jit(solution)/shard_map/all_gather | solution.py:88
  111.9 10.4 %fusion = f32[8,4,36,2,448]{4,2,3,1,0:T(8,128)S(1)} fusion(bf16[8,4,36,2560,1]{3,1,2,0,4:T(4,128)(2,1)} %bitcast.78, bf16[1,2560,2,448]{1,3,2,0:T(8,128)(2,1)} %param.15), kind=kOutput, calls=%fused_computation.3 | convolution fusion | flops 5284823040 | bytes 14614528 | tf_op jit(solution)/shard_map/...d,dgf->...gf/dot_general | solution.py:86
  122.2 5.7 %convolution_convert_fusion = bf16[8,4,36,2560]{3,2,1,0:T(8,128)(2,1)} fusion(bf16[1,448,2560]{2,1,0:T(8,128)(2,1)S(1)} %copy-done, f32[8,4,36,2,448]{4,2,3,1,0:T(8,128)S(1)} %fusion), kind=kOutput, calls=%fused_computation.5 | convolution fusion | flops 2648457216 | bytes 12320768 | tf_op jit(solution)/shard_map/...f,fd->...d/dot_general | solution.py:94
  127.9 76.4 %reduce-scatter.2.cloned.1.call-done = bf16[1,4,36,2560]{3,2,1,0:T(8,128)(2,1)} async-done(((bf16[8,4,36,2560]{3,2,1,0:T(8,128)(2,1)}), bf16[1,4,36,2560]{3,2,1,0:T(8,128)(2,1)}) %reduce-scatter.2.cloned.1.call-update) | async-done | bytes 737296 | tf_op jit(solution)/shard_map/reduce_scatter | solution.py:93
  204.4 4.2 %all-to-all-start.2 = ((bf16[4,36,2560]{2,1,0:T(8,128)(2,1)}), bf16[4,36,2560]{2,1,0:T(8,128)(2,1)S(1)}, u32[]{:S(2)}, u32[]{:S(2)}) async-start(bf16[4,36,2560]{2,1,0:T(8,128)(2,1)} %bitcast.75), calls=%async_computation.3 | async-start | bytes 1638400 | tf_op jit(solution)/shard_map/all_to_all | solution.py:101
  208.7 10.9 %all-to-all-done.2 = bf16[4,36,2560]{2,1,0:T(8,128)(2,1)S(1)} async-done(((bf16[4,36,2560]{2,1,0:T(8,128)(2,1)}), bf16[4,36,2560]{2,1,0:T(8,128)(2,1)S(1)}, u32[]{:S(2)}, u32[]{:S(2)}) %all-to-all-start.2) | async-done | bytes 737312 | tf_op jit(solution)/shard_map/all_to_all | solution.py:101
  219.6 1.3 reshape.166
  220.9 2.7 gather_fusion
  223.6 1.5 reshape.159
  225.2 2.6 multiply_reduce_fusion
  227.9 0.9 fusion.18
  228.8 1.4 broadcast_in_dim.5
  230.3 4.3 %all-to-all-start.3 = ((bf16[8,48,2560]{2,1,0:T(8,128)(2,1)}), bf16[8,48,2560]{2,1,0:T(8,128)(2,1)}, u32[]{:S(2)}, u32[]{:S(2)}) async-start(bf16[8,48,2560]{2,1,0:T(8,128)(2,1)} %broadcast_in_dim.5), calls=%async_computation.4 | async-start | bytes 3932160 | tf_op jit(solution)/shard_map/all_to_all | solution.py:41
  234.6 6.3 %copy.56 = bf16[3,256,2560]{2,1,0:T(8,128)(2,1)} copy(bf16[3,256,2560]{1,2,0:T(8,128)(2,1)} %bitcast.70) | data formatting | bytes 7864320 | tf_op jit(solution)/shard_map/nd,dgc->ngc/dot_general | solution.py:116
  240.9 39.4 %all-to-all-done.3 = bf16[8,48,2560]{2,1,0:T(8,128)(2,1)} async-done(((bf16[8,48,2560]{2,1,0:T(8,128)(2,1)}), bf16[8,48,2560]{2,1,0:T(8,128)(2,1)}, u32[]{:S(2)}, u32[]{:S(2)}) %all-to-all-start.3) | async-done | bytes 1966112 | tf_op jit(solution)/shard_map/all_to_all | solution.py:41
  280.3 4.9 %fusion.34 = f32[384,3,2,128]{0,3,2,1:T(8,128)S(1)} fusion(bf16[384,2560,1,1]{1,0,3,2:T(8,128)(2,1)} %bitcast.14, bf16[3,2,128,2560]{3,2,1,0:T(8,128)(2,1)} %bitcast.71), kind=kOutput, calls=%fused_computation.71 | convolution fusion | flops 1509949440 | bytes 7077888 | tf_op jit(solution)/shard_map/nd,dgc->ngc/dot_general | solution.py:116
  285.4 11.2 %all_gather.11 = bf16[1536,256]{0,1:T(8,128)(2,1)S(1)} all-gather(bf16[384,256]{0,1:T(8,128)(2,1)S(1)} %bitcast.77), channel_id=1, replica_groups=mesh['set'=8,'exp_0'=2,'exp_1'=2,'seq'=8] {'exp_0','exp_1'}, dimensions={0}, use_global_device_ids=true | all-gather | bytes 983040 | tf_op jit(solution)/shard_map/all_gather | solution.py:125
  296.7 8.7 %all_gather.10 = bf16[1536,256]{0,1:T(8,128)(2,1)S(1)} all-gather(bf16[384,256]{0,1:T(8,128)(2,1)S(1)} %bitcast.76), channel_id=1, replica_groups=mesh['set'=8,'exp_0'=2,'exp_1'=2,'seq'=8] {'exp_0','exp_1'}, dimensions={0}, use_global_device_ids=true | all-gather | bytes 983040 | tf_op jit(solution)/shard_map/all_gather | solution.py:126
  305.4 1.0 bitcast_reduce_fusion
  306.3 0.8 fusion.11
  307.7 0.7 convolution_convert_fusion.1
  308.3 51.3 %all_to_all.27 = bf16[8,48,2560]{2,1,0:T(8,128)(2,1)S(1)} all-to-all(bf16[8,48,2560]{2,1,0:T(8,128)(2,1)S(1)} %bitcast.69), channel_id=1, replica_groups=mesh['set'=8,'exp_0'=2,'exp_1'=2,'seq'=8] {'seq'}, dimensions={0} | all-to-all | bytes 3932160 | tf_op jit(solution)/shard_map/all_to_all | solution.py:52
  359.9 0.8 fusion.19
  (43 shorter events, 3.9 us)
Async XLA Ops:
  7.2 115.1 %copy-start = (bf16[1,448,2560]{2,1,0:T(8,128)(2,1)S(1)}, bf16[1,448,2560]{2,1,0:T(8,128)(2,1)}, u32[]{:S(2)}) copy-start(bf16[1,448,2560]{2,1,0:T(8,128)(2,1)} %param.16) | copy-start | bytes 6881284
  7.2 104.7 %all-gather.2.cloned.1.call-start = ((), (), s32[]{:S(2)}) async-start(), calls=%async_computation.6 | async-start | bytes 6635520 | tf_op jit(solution)/shard_map/all_gather | solution.py:88
  39.3 165.1 %reduce-scatter.2.cloned.1.call-start = ((), (), s32[]{:S(2)}) async-start(), calls=%async_computation.7 | async-start | bytes 7372800 | tf_op jit(solution)/shard_map/reduce_scatter | solution.py:93
  127.9 80.7 %copy-start.4 = (s32[48,2]{0,1:T(2,128)S(1)}, s32[48,2]{0,1:T(2,128)}, u32[]{:S(2)}) copy-start(s32[48,2]{0,1:T(2,128)} %param.13) | copy-start | bytes 1156
  204.4 15.2 %all-to-all-start.2 = ((bf16[4,36,2560]{2,1,0:T(8,128)(2,1)}), bf16[4,36,2560]{2,1,0:T(8,128)(2,1)S(1)}, u32[]{:S(2)}, u32[]{:S(2)}) async-start(bf16[4,36,2560]{2,1,0:T(8,128)(2,1)} %bitcast.75), calls=%async_computation.3 | async-start | bytes 1638400 | tf_op jit(solution)/shard_map/all_to_all | solution.py:101
  223.6 4.1 %copy-start.1 = (bf16[48,2560]{1,0:T(8,128)(2,1)S(1)}, bf16[48,2560]{1,0:T(8,128)(2,1)}, u32[]{:S(2)}) copy-start(bf16[48,2560]{1,0:T(8,128)(2,1)} %param.11) | copy-start | bytes 737284
  227.9 132.0 %copy-start.2 = (bf16[48,2560]{1,0:T(8,128)(2,1)}, bf16[48,2560]{1,0:T(8,128)(2,1)S(1)}, u32[]{:S(2)}) copy-start(bf16[48,2560]{1,0:T(8,128)(2,1)S(1)} %get-tuple-element.5) | copy-start | bytes 737284
  230.3 50.0 %all-to-all-start.3 = ((bf16[8,48,2560]{2,1,0:T(8,128)(2,1)}), bf16[8,48,2560]{2,1,0:T(8,128)(2,1)}, u32[]{:S(2)}, u32[]{:S(2)}) async-start(bf16[8,48,2560]{2,1,0:T(8,128)(2,1)} %broadcast_in_dim.5), calls=%async_computation.4 | async-start | bytes 3932160 | tf_op jit(solution)/shard_map/all_to_all | solution.py:41
  280.3 5.1 %copy-start.6 = (f32[128]{0:T(128)S(1)}, f32[128]{0:T(128)}, u32[]{:S(2)}) copy-start(f32[128]{0:T(128)} %param.20) | copy-start | bytes 1540
  285.2 20.2 %copy-start.5 = (f32[128]{0:T(128)S(1)}, f32[128]{0:T(128)}, u32[]{:S(2)}) copy-start(f32[128]{0:T(128)} %param.19) | copy-start | bytes 1540
  306.3 1.3 copy-start.3
Sparse Core Ops, SparseCore 0:
  39.4 72.3 all-gather.1
  128.1 76.2 reduce-scatter.1
where the time goes:
time: 368 us
  waiting for transfers between devices  199 us (54%)
  blocking collectives  90.7 us (25%)
  matrix products  23.4 us (6%)
  local copies, waits for them, and re-layouts  23.1 us (6%)
  between operations  14.3 us (4%)
  starting transfers between devices  8.64 us (2%)
  other arithmetic  8.14 us (2%)
    reduce_scatter x1, waiting for transfers between devices, shards(): lax.psum_scatter(jnp.einsum('...f,fd->...d', hidden_all, w_down[0], prefe...  76.4 us
    all_gather x1, waiting for transfers between devices, shards(): lax.all_gather(received[None], 'seq', axis=0, tiled=True)  72.5 us
    all_to_all x1, blocking collectives, summed_on_arrival(): lax.all_to_all(cut_along(value, dim, length), axis, 0, 0, tiled=True)  51.3 us
    all_to_all x1, waiting for transfers between devices, from_everyone(): lax.all_to_all(jnp.broadcast_to(value[None], (length, *value.shape)), axi...  39.4 us
    all_to_all x2, blocking collectives, moved_by_axis(): filled = lax.all_to_all(filled, axes[k], k, k, tiled=True)  19.5 us
    all_gather x1, blocking collectives, shards(): key_piece = lax.all_gather(projected[:, 1], EXP, axis=0, tiled=True)  11.2 us
    all_to_all x1, waiting for transfers between devices, shards(): lax.all_to_all(summed[0].astype(jnp.bfloat16), EXP, split_axis=0, concat_...  10.9 us
    dot_general x1, matrix products, shards(): jnp.einsum('...d,dgf->...gf', lax.all_gather(received[None], 'seq', axis=...  10.4 us
  transfers between devices with their start and end apart: 4, of which 4 were waited for; matrix products, arithmetic and copies ran while one was open for 2% of the time, Pallas kernels for 0%

commit v1 on v0

--- a/solution.py
+++ b/solution.py
@@ -85,7 +85,9 @@
     received = two_step_exchange(dispatch, ("exp_0", "exp_1"), (1, 0), 0, 0)
     gate_up = jnp.einsum(
         "...d,dgf->...gf",
-        lax.all_gather(received[None], "seq", axis=0, tiled=True),
+        jnp.concatenate(
+            lax.all_to_all(jnp.stack([received[None]] * lax.axis_size("seq")), "seq", 0, 0), axis=0
+        ),
         w_gate_up[0],
         preferred_element_type=jnp.float32,
     )

time: 368 us -> 427 us (1.16)
  blocking collectives: 90.7 us -> 225 us
  waiting for transfers between devices: 199 us -> 130 us
    all_to_all x0 -> x1, blocking collectives: none -> 137 us  [shards(): lax.all_to_all(jnp.stack([received[None]] * lax.axis_size('seq')), 'seq',...]
    all_gather x1 -> x0, waiting for transfers between devices: 72.5 us -> none  [shards(): lax.all_gather(received[None], 'seq', axis=0, tiled=True)]
  transfers between devices with their start and end apart: 4 -> 3, of which waited for: 4 -> 3; matrix products, arithmetic and copies ran while one was open for 2% -> 1% of each run, Pallas kernels for 0% -> 0%
where the time goes in v1:
time: 427 us; the launch traced here: 426 us
  blocking collectives  225 us (53%)
  waiting for transfers between devices  130 us (30%)
  local copies, waits for them, and re-layouts  22.8 us (5%)
  matrix products  19.6 us (5%)
  between operations  14.3 us (3%)
  starting transfers between devices  8.31 us (2%)
  other arithmetic  6.16 us (1%)
    all_to_all x1, blocking collectives, shards(): lax.all_to_all(jnp.stack([received[None]] * lax.axis_size('seq')), 'seq',...  137 us
    reduce_scatter x1, waiting for transfers between devices, shards(): lax.psum_scatter(jnp.einsum('...f,fd->...d', hidden_all, w_down[0], prefe...  76.7 us
    all_to_all x1, blocking collectives, summed_on_arrival(): lax.all_to_all(cut_along(value, dim, length), axis, 0, 0, tiled=True)  51.4 us
    all_to_all x1, waiting for transfers between devices, from_everyone(): lax.all_to_all(jnp.broadcast_to(value[None], (length, *value.shape)), axi...  42.6 us
    all_to_all x2, blocking collectives, moved_by_axis(): filled = lax.all_to_all(filled, axes[k], k, k, tiled=True)  19.5 us
    all_to_all x1, waiting for transfers between devices, shards(): lax.all_to_all(summed[0].astype(jnp.bfloat16), EXP, split_axis=0, concat_...  10.9 us
    all_gather x1, blocking collectives, shards(): key_piece = lax.all_gather(projected[:, 1], EXP, axis=0, tiled=True)  8.71 us
    all_gather x1, blocking collectives, shards(): value_piece = lax.all_gather(projected[:, 2], EXP, axis=0, tiled=True)  8.7 us
  transfers between devices with their start and end apart: 3, of which 3 were waited for; matrix products, arithmetic and copies ran while one was open for 1% of the time, Pallas kernels for 0%

profile of v1, /device:TPU:1, one launch (start us, length us, event | category | flops | bytes accessed | tf_op | source)
XLA Modules:
  0.0 426.5 jit_solution(8484641740254395847)
XLA Ops:
  7.2 0.9 copy.38
  8.1 0.7 broadcast_multiply_fusion
  9.6 1.1 fusion.13
  10.7 1.1 fusion.15
  11.8 3.7 scatter_custom_fusion
  15.5 1.3 reshape_reshape_reshape.3
  16.8 0.8 copy.39
  17.5 7.1 %all_to_all.30 = bf16[2,2,1,36,2560]{4,0,3,2,1:T(2,128)(2,1)S(1)} all-to-all(bf16[2,2,1,36,2560]{4,0,3,2,1:T(2,128)(2,1)S(1)} %copy.39), channel_id=1, replica_groups=mesh['set'=8,'exp_0'=2,'exp_1'=2,'seq'=8] {'exp_1'}, dimensions={1} | all-to-all | bytes 1474560 | tf_op jit(solution)/shard_map/all_to_all | solution.py:29
  25.2 12.4 %all_to_all.31 = bf16[2,2,1,36,2560]{4,1,3,2,0:T(2,128)(2,1)S(1)} all-to-all(bf16[2,2,1,36,2560]{4,1,3,2,0:T(2,128)(2,1)S(1)} %copy.40), channel_id=1, replica_groups=mesh['set'=8,'exp_0'=2,'exp_1'=2,'seq'=8] {'exp_0'}, dimensions={0} | all-to-all | bytes 1474560 | tf_op jit(solution)/shard_map/all_to_all | solution.py:29
  37.6 1.4 copy.41
  39.0 2.4 stack_broadcast_in_dim_reshape_reshape.2
  41.4 1.5 stack.2
  42.9 136.7 %all_to_all.32 = bf16[8,1,4,36,2560]{4,2,3,1,0:T(4,128)(2,1)S(1)} all-to-all(bf16[8,1,4,36,2560]{4,2,3,1,0:T(4,128)(2,1)S(1)} %stack.2), channel_id=1, replica_groups=mesh['set'=8,'exp_0'=2,'exp_1'=2,'seq'=8] {'seq'}, dimensions={0} | all-to-all | bytes 11796480 | tf_op jit(solution)/shard_map/all_to_all | solution.py:89
  179.6 7.1 %fusion = f32[8,4,36,2,448]{4,2,3,1,0:T(8,128)S(1)} fusion(bf16[8,1,4,36,2560]{4,2,3,1,0:T(4,128)(2,1)S(1)} %all_to_all.32, bf16[1,2560,2,448]{1,3,2,0:T(8,128)(2,1)S(1)} %bitcast.85), kind=kOutput, calls=%fused_computation.3 | convolution fusion | flops 5284823040 | bytes 14614528 | tf_op jit(solution)/shard_map/...d,dgf->...gf/dot_general | solution.py:86
  186.8 5.7 %convolution_convert_fusion = bf16[8,4,36,2560]{3,2,1,0:T(8,128)(2,1)} fusion(bf16[1,448,2560]{2,1,0:T(8,128)(2,1)S(1)} %copy-done, f32[8,4,36,2,448]{4,2,3,1,0:T(8,128)S(1)} %fusion), kind=kOutput, calls=%fused_computation.6 | convolution fusion | flops 2648457216 | bytes 12320768 | tf_op jit(solution)/shard_map/...f,fd->...d/dot_general | solution.py:96
  192.5 76.7 %reduce-scatter.2.cloned.1.call-done = bf16[1,4,36,2560]{3,2,1,0:T(8,128)(2,1)} async-done(((bf16[8,4,36,2560]{3,2,1,0:T(8,128)(2,1)}), bf16[1,4,36,2560]{3,2,1,0:T(8,128)(2,1)}) %reduce-scatter.2.cloned.1.call-update) | async-done | bytes 737296 | tf_op jit(solution)/shard_map/reduce_scatter | solution.py:95
  269.2 4.2 all-to-all-start.3
  273.5 10.9 %all-to-all-done.3 = bf16[4,36,2560]{2,1,0:T(8,128)(2,1)S(1)} async-done(((bf16[4,36,2560]{2,1,0:T(8,128)(2,1)}), bf16[4,36,2560]{2,1,0:T(8,128)(2,1)S(1)}, u32[]{:S(2)}, u32[]{:S(2)}) %all-to-all-start.3) | async-done | bytes 737312 | tf_op jit(solution)/shard_map/all_to_all | solution.py:103
  284.5 0.9 gather_fusion
  286.1 1.3 multiply_reduce_fusion
  287.7 1.5 broadcast_in_dim.5
  289.2 4.1 all-to-all-start.4
  293.3 6.2 %copy.54 = bf16[3,256,2560]{2,1,0:T(8,128)(2,1)} copy(bf16[3,256,2560]{1,2,0:T(8,128)(2,1)} %bitcast.75) | data formatting | bytes 7864320 | tf_op jit(solution)/shard_map/nd,dgc->ngc/dot_general | solution.py:118
  299.5 42.6 %all-to-all-done.4 = bf16[8,48,2560]{2,1,0:T(8,128)(2,1)S(1)} async-done(((bf16[8,48,2560]{2,1,0:T(8,128)(2,1)}), bf16[8,48,2560]{2,1,0:T(8,128)(2,1)S(1)}, u32[]{:S(2)}, u32[]{:S(2)}) %all-to-all-start.4) | async-done | bytes 1966112 | tf_op jit(solution)/shard_map/all_to_all | solution.py:41
  342.1 4.3 %fusion.35 = f32[384,3,2,128]{0,3,2,1:T(8,128)S(1)} fusion(bf16[384,2560,1,1]{1,0,3,2:T(8,128)(2,1)S(1)} %bitcast.79, bf16[3,2,128,2560]{3,2,1,0:T(8,128)(2,1)} %bitcast.76), kind=kOutput, calls=%fused_computation.72 | convolution fusion | flops 1509949440 | bytes 7077888 | tf_op jit(solution)/shard_map/nd,dgc->ngc/dot_general | solution.py:118
  346.7 8.7 %all_gather.7 = bf16[1536,256]{0,1:T(8,128)(2,1)S(1)} all-gather(bf16[384,256]{0,1:T(8,128)(2,1)S(1)} %bitcast.83), channel_id=1, replica_groups=mesh['set'=8,'exp_0'=2,'exp_1'=2,'seq'=8] {'exp_0','exp_1'}, dimensions={0}, use_global_device_ids=true | all-gather | bytes 983040 | tf_op jit(solution)/shard_map/all_gather | solution.py:127
  355.4 8.7 %all_gather.6 = bf16[1536,256]{0,1:T(8,128)(2,1)S(1)} all-gather(bf16[384,256]{0,1:T(8,128)(2,1)S(1)} %bitcast.82), channel_id=1, replica_groups=mesh['set'=8,'exp_0'=2,'exp_1'=2,'seq'=8] {'exp_0','exp_1'}, dimensions={0}, use_global_device_ids=true | all-gather | bytes 983040 | tf_op jit(solution)/shard_map/all_gather | solution.py:128
  364.1 1.0 bitcast_reduce_fusion
  365.1 0.8 fusion.12
  366.4 0.7 convolution_convert_fusion.1
  367.1 51.4 %all_to_all.33 = bf16[8,48,2560]{2,1,0:T(8,128)(2,1)S(1)} all-to-all(bf16[8,48,2560]{2,1,0:T(8,128)(2,1)S(1)} %bitcast.74), channel_id=1, replica_groups=mesh['set'=8,'exp_0'=2,'exp_1'=2,'seq'=8] {'seq'}, dimensions={0} | all-to-all | bytes 3932160 | tf_op jit(solution)/shard_map/all_to_all | solution.py:52
  418.9 0.8 fusion.20
  (51 shorter events, 3.6 us)
Async XLA Ops:
  7.2 179.6 %copy-start = (bf16[1,448,2560]{2,1,0:T(8,128)(2,1)S(1)}, bf16[1,448,2560]{2,1,0:T(8,128)(2,1)}, u32[]{:S(2)}) copy-start(bf16[1,448,2560]{2,1,0:T(8,128)(2,1)} %param.16) | copy-start | bytes 6881284
  7.2 262.0 %reduce-scatter.2.cloned.1.call-start = ((), (), s32[]{:S(2)}) async-start(), calls=%async_computation.7 | async-start | bytes 7372800 | tf_op jit(solution)/shard_map/reduce_scatter | solution.py:95
  41.4 138.3 %slice-start = ((s8[4587520]{0:T(1024)(128)(4,1)}), s8[4194304]{0:T(1024)(128)(4,1)S(1)}, s32[]{:S(2)}) async-start(s8[4587520]{0:T(1024)(128)(4,1)} %bitcast.84), calls=%async_computation.8 | async-start | bytes 8388608
  42.9 136.7 %slice-start.1 = ((s8[4587520]{0:T(1024)(128)(4,1)}), s8[393216]{0:T(1024)(128)(4,1)S(1)}, s32[]{:S(2)}) async-start(s8[4587520]{0:T(1024)(128)(4,1)} %bitcast.84), calls=%async_computation.9 | async-start | bytes 786432
  192.4 80.9 %copy-start.6 = (s32[48,2]{0,1:T(2,128)S(1)}, s32[48,2]{0,1:T(2,128)}, u32[]{:S(2)}) copy-start(s32[48,2]{0,1:T(2,128)} %param.13) | copy-start | bytes 1156
  269.2 15.2 %all-to-all-start.3 = ((bf16[4,36,2560]{2,1,0:T(8,128)(2,1)}), bf16[4,36,2560]{2,1,0:T(8,128)(2,1)S(1)}, u32[]{:S(2)}, u32[]{:S(2)}) async-start(bf16[4,36,2560]{2,1,0:T(8,128)(2,1)} %bitcast.81), calls=%async_computation.4 | async-start | bytes 1638400 | tf_op jit(solution)/shard_map/all_to_all | solution.py:103
  285.4 1.9 copy-start.2
  285.5 2.1 copy-start.5
  287.6 131.3 %copy-start.3 = (bf16[48,2560]{1,0:T(8,128)(2,1)}, bf16[48,2560]{1,0:T(8,128)(2,1)S(1)}, u32[]{:S(2)}) copy-start(bf16[48,2560]{1,0:T(8,128)(2,1)S(1)} %get-tuple-element.5) | copy-start | bytes 737284
  289.2 52.9 %all-to-all-start.4 = ((bf16[8,48,2560]{2,1,0:T(8,128)(2,1)}), bf16[8,48,2560]{2,1,0:T(8,128)(2,1)S(1)}, u32[]{:S(2)}, u32[]{:S(2)}) async-start(bf16[8,48,2560]{2,1,0:T(8,128)(2,1)} %broadcast_in_dim.5), calls=%async_computation.5 | async-start | bytes 3932160 | tf_op jit(solution)/shard_map/all_to_all | solution.py:41
  342.1 4.5 %copy-start.8 = (f32[128]{0:T(128)S(1)}, f32[128]{0:T(128)}, u32[]{:S(2)}) copy-start(f32[128]{0:T(128)} %param.20) | copy-start | bytes 1540
  346.5 17.7 %copy-start.7 = (f32[128]{0:T(128)S(1)}, f32[128]{0:T(128)}, u32[]{:S(2)}) copy-start(f32[128]{0:T(128)} %param.19) | copy-start | bytes 1540
  365.1 1.3 copy-start.4
  367.1 52.5 %copy-start.1 = (bf16[1,448,2560]{2,1,0:T(8,128)(2,1)S(1)}, bf16[1,448,2560]{2,1,0:T(8,128)(2,1)}, u32[]{:S(2)}) copy-start(bf16[1,448,2560]{2,1,0:T(8,128)(2,1)} %param.16) | copy-start | bytes 6881284
Sparse Core Ops, SparseCore 0:
  192.6 76.5 reduce-scatter.1
